TPU v7x, 128 devices: a whole 4x4x4 slice. The times are simulated.
128 devices in a mesh: grp: 8 (over x, y_lo), tp: 16 (over z, y_hi, core).
Axes of the slice: x: 4, y: 4 (y_hi: 2, y_lo: 2; y = y_hi * 2 + y_lo), z: 4, core: 2. Of those that a mesh axis runs over, the one named last changes fastest.
Arguments:
- vision_in: bfloat16 [4096, 3200], P(('grp', 'tp')), may hold values from -6 to 6
- vis_gain: float32 [3200], replicated, may hold values from 0.5 to 2
- first_weight: bfloat16 [3200, 12800], P(None, 'tp'), may hold values from -0.109375 to 0.109375
- second_weight: bfloat16 [12800, 3200], P('tp'), may hold values from -0.0546875 to 0.0546875
- layer_scale: float32 [3200], replicated, may hold values from 0.3 to 1.5
- proj_gain: float32 [12800], replicated, may hold values from 0.5 to 2
- proj_weight: bfloat16 [12800, 8192], P(None, 'tp'), may hold values from -0.0546875 to 0.0546875
- text_embed: bfloat16 [9216, 8192], P('grp', 'tp'), may hold values from -6 to 6
- dest_row: int32 [1024], replicated, may hold values from 0 to 9215, as said below
- cotangent: bfloat16 [9216, 8192], P('grp', 'tp'), may hold values from -6 to 6
Outputs:
- seq_embed: bfloat16 [9216, 8192], P('grp', 'tp')
- grad_vision: bfloat16 [4096, 3200], P(('grp', 'tp'))
Inputs may be any that keep to these rules, and one draw needn't show every extreme that they name: `dest_row`: all values distinct. Sequence h is rows h * 1152 to (h + 1) * 1152 - 1. The 128 merged rows of index g of grp form four images of 32 rows each; each image fills consecutive token rows of its own sequence, four different sequences for one index of grp, inside positions g * (144) to (g + 1) * 144 - 1 of that sequence. Image j of index g goes to sequence (g + k_j) mod 8 with four distinct shifts k_j common to all g, among them 1 and 4; so at most, and exactly, 32 rows go from one index of grp to one sequence, and every sequence receives four images from four different indices of grp.
All inputs are finite; a program needn't handle non-finite values.
Results may differ from a plain program's by a relative error of at most 0.025.
Values may be sent and summed in bfloat16 or wider, within the bound.
A program may use at most 128 MiB of HBM per device.

v0:
```python
import functools

import jax
import jax.numpy as jnp
from jax import lax
from jax.experimental import pallas as pl
from jax.experimental.pallas import tpu as pltpu
from jax.sharding import Mesh
from jax.sharding import PartitionSpec as P

AXES = ("x", "ylo", "z", "yhi", "core")
GRP = ("x", "ylo")
TP = ("z", "yhi", "core")
MESH = pl.DeviceIdType.MESH
VIS_EPS = 1e-06
PROJ_EPS = 1e-05
F32 = jnp.float32
BF16 = jnp.bfloat16

PLACES = [(0, 0), (1, 0), (-1, 0), (0, 1), (2, 0), (1, 1), (-1, 1), (2, 1)]
PAIR = {place: n for n, place in enumerate(PLACES)}
PAIRS = 8
UNITS = 16
NEAR = (0, 5)
FAR = (5, 8)
QUARTERS = (0, 3, 1, 2)
AG_MSGS = 29
RS_MSGS = 32
PHASE_MSGS = AG_MSGS + RS_MSGS


def erf_half(u):
    return 0.5 * (1.0 + lax.erf(u * 0.7071067811865476))


def gelu(u):
    return u * erf_half(u)


def gelu_slope(u):
    return erf_half(u) + u * (jnp.exp(-0.5 * u * u) * 0.3989422804014327)


def dot(a, b):
    return jnp.dot(a, b, preferred_element_type=F32)


def dot_t(a, b):
    return lax.dot_general(a, b, (((1,), (1,)), ((), ())), preferred_element_type=F32)


def iota(shape, dim):
    return lax.broadcasted_iota(jnp.int32, shape, dim)


def one_hot(cond):
    return jnp.where(cond, 1.0, 0.0).astype(BF16)


def line(ref, start, count):
    return jnp.concatenate([ref[pl.ds(start + n, 1), :] for n in range(count)], axis=1)


def turned(col):
    n = col.shape[0]
    return jnp.sum(jnp.where(iota((n, n), 0) == iota((n, n), 1), col, 0.0), 0, keepdims=True)


def kernel(
    x_ref, vgain_ref, ls_ref, pgain_ref, dest_ref,
    w1_hbm, w2_hbm, wp_hbm, text_hbm, cot_hbm,
    seq_hbm, grad_ref,
    w1, w2, wp, cot, seq,
    g1, g2, g3, part, rcore, rya, rye, rzb, rzc, rzd,
    pre1, hid, pre2, hid2,
    out_slots, arrived, picked, returned,
    xhat, xinv, own, mhat, minv, vgain, ls, pgain,
    scol, srow, tcol, trow,
    ssem, rsem, esend, erecv, lsem,
):
    x = lax.axis_index("x")
    ylo = lax.axis_index("ylo")
    z = lax.axis_index("z")
    yhi = lax.axis_index("yhi")
    core = lax.axis_index("core")
    grp = 2 * x + ylo
    unit_rows, width = x_ref.shape
    half = unit_rows // 2
    merged_own = unit_rows // 4
    merged_all = UNITS * merged_own
    slots = 8 * 32
    seq_len = cot.shape[0]
    to = {
        "y": {"ylo": 1 - ylo, "yhi": 1 - yhi},
        "z+": {"z": lax.rem(z + 1, 4)},
        "z-": {"z": lax.rem(z + 3, 4)},
        "c": {"core": 1 - core},
    }

    def peer(k):
        g = lax.rem(grp + k, 8)
        return g, {"x": g // 2, "ylo": lax.rem(g, 2)}

    barrier = pltpu.get_barrier_semaphore()
    for d in to.values():
        pl.semaphore_signal(barrier, inc=1, device_id=d, device_id_type=MESH)
    for k in range(1, 8):
        pl.semaphore_signal(barrier, inc=1, device_id=peer(k)[1], device_id_type=MESH)

    loads = []
    for n, (src, dst) in enumerate(((cot_hbm, cot), (w1_hbm, w1), (w2_hbm, w2), (wp_hbm, wp), (text_hbm, seq))):
        copy = pltpu.make_async_copy(src, dst, lsem.at[n])
        copy.start()
        loads.append(copy)
    cot_load, w1_load, w2_load, wp_load, text_load = loads

    sent = []

    def remote(src, dst, where, n):
        copy = pltpu.make_async_remote_copy(
            src_ref=src, dst_ref=dst, send_sem=ssem.at[n], recv_sem=rsem.at[n],
            device_id=to[where], device_id_type=MESH,
        )
        sent.append(copy)
        return copy

    def free_part():
        for copy in sent:
            copy.wait_send()
        sent.clear()

    def halves(h):
        return pl.ds(h * half, half)

    def quarter(q):
        return pl.ds(q * merged_own, merged_own)

    def gather(phase, buf, early, middle, late):
        count = iter(range(phase * PHASE_MSGS, phase * PHASE_MSGS + AG_MSGS))

        def msg(src, dst, where, rows=None):
            s, d = buf.at[PAIR[src]], buf.at[PAIR[dst]]
            if rows is not None:
                s, d = s.at[rows], d.at[rows]
            return remote(s, d, where, next(count))

        def cross(first, last):
            return remote(buf.at[first:last], buf.at[PAIRS + first : PAIRS + last], "c", next(count))

        own_zp = [msg((0, 0), (-1, 0), "z+", quarter(q)) for q in range(4)]
        own_zm = [msg((0, 0), (1, 0), "z-", quarter(q)) for q in range(4)]
        own_y = [msg((0, 0), (0, 1), "y", halves(h)) for h in range(2)]
        two = {q: msg((-1, 0), (2, 0), "z+", quarter(q)) for q in (0, 1)}
        two |= {q: msg((1, 0), (2, 0), "z-", quarter(q)) for q in (3, 2)}
        y_zp = [msg((0, 1), (-1, 1), "z+", halves(h)) for h in range(2)]
        y_zm = [msg((0, 1), (1, 1), "z-", halves(h)) for h in range(2)]
        two_y = [msg((2, 0), (2, 1), "y", quarter(q)) for q in range(4)]
        c_own, c_side, c_y, c_two, c_far, c_last = (
            cross(*r) for r in ((0, 1), (1, 3), (3, 4), (4, 5), (5, 7), (7, 8))
        )
        for copy in (
            own_zp[0], own_zm[3], own_y[0], own_zp[1], own_zm[2], own_y[1], own_zp[2], own_zm[1], c_own,
        ):
            copy.start()
        early()
        for p, m in ((0, 3), (1, 2)):
            own_zp[p].wait_recv()
            two[p].start()
            own_zm[m].wait_recv()
            two[m].start()
        own_zp[3].start()
        own_zm[0].start()
        own_y[0].wait_recv()
        y_zp[0].start()
        y_zm[0].start()
        for q in (0, 3):
            two[q].wait_recv()
            two_y[q].start()
        own_y[1].wait_recv()
        y_zp[1].start()
        y_zm[1].start()
        c_y.start()
        for q in (1, 2):
            two[q].wait_recv()
            two_y[q].start()
        c_two.start()
        for copy in (own_zp[2], own_zp[3], own_zm[1], own_zm[0]):
            copy.wait_recv()
        c_side.start()
        for copy in (c_own, c_y, c_two, c_side):
            copy.wait_recv()
        middle()
        for copy in (*y_zp, *y_zm):
            copy.wait_recv()
        c_far.start()
        for copy in two_y:
            copy.wait_recv()
        c_last.start()
        c_far.wait_recv()
        c_last.wait_recv()
        late()

    class Scatter:
        def __init__(self, phase):
            count = iter(range(phase * PHASE_MSGS + AG_MSGS, (phase + 1) * PHASE_MSGS))
            self.phase = phase

            def msg(place, rows, dst, where):
                return remote(part.at[PAIR[place], rows], dst.at[rows], where, next(count))

            def cross(first, last, rows):
                return remote(
                    part.at[PAIRS + first : PAIRS + last, rows], rcore.at[phase, first:last, rows], "c", next(count)
                )

            if phase == 1:
                self.cross = [cross(0, PAIRS, quarter(q)) for q in range(4)]
            else:
                everything = pl.ds(0, unit_rows)
                self.cross = {g: cross(*g, everything) for g in (FAR, NEAR)}
            self.a = [msg((2, 1), quarter(q), rya.at[phase], "y") for q in range(4)]
            self.b = [
                (msg((1, 1), quarter(q), rzb.at[phase, 0], "z+"), msg((-1, 1), quarter(q), rzb.at[phase, 1], "z-"))
                for q in range(4)
            ]
            self.c = [msg((2, 0), quarter(q), rzc.at[phase], "z+" if q < 2 else "z-") for q in range(4)]
            self.dp = [msg((1, 0), quarter(q), rzd.at[phase, 0], "z+") for q in range(4)]
            self.dm = [msg((-1, 0), quarter(q), rzd.at[phase, 1], "z-") for q in range(4)]
            self.e = [msg((0, 1), halves(h), rye.at[phase], "y") for h in range(2)]

        def join(self, first, last, rows):
            for n in range(first, last):
                v = part[n, rows, :].astype(F32) + rcore[self.phase, n, rows, :].astype(F32)
                part[n, rows, :] = v.astype(BF16)

        def add(self, place, rows, *refs):
            n = PAIR[place]
            v = part[n, rows, :].astype(F32)
            for ref in refs:
                v = v + ref[rows, :].astype(F32)
            part[n, rows, :] = v.astype(BF16)

        def leave(self, q):
            self.a[q].start()
            for copy in self.b[q]:
                copy.start()

        def relay(self, idle):
            p = self.phase

            def pass_two(q):
                self.a[q].wait_recv()
                self.add((2, 0), quarter(q), rya.at[p])
                self.c[q].start()

            def pass_y(h):
                for q in (2 * h, 2 * h + 1):
                    for copy in self.b[q]:
                        copy.wait_recv()
                self.add((0, 1), halves(h), rzb.at[p, 0], rzb.at[p, 1])
                self.e[h].start()

            pass_two(0)
            pass_two(3)
            pass_y(0)
            pass_two(1)
            pass_two(2)
            for q in (2, 3):
                self.dp[q].start()
            for q in (1, 0):
                self.dm[q].start()
            pass_y(1)
            for q in QUARTERS:
                self.c[q].wait_recv()
                side, out = ((1, 0), self.dp) if q < 2 else ((-1, 0), self.dm)
                self.add(side, quarter(q), rzc.at[p])
                out[q].start()
            idle()
            for copy in (*self.e, *self.dp, *self.dm):
                copy.wait_recv()
            return (
                part[0].astype(F32) + rzd[p, 0].astype(F32) + rzd[p, 1].astype(F32) + rye[p].astype(F32)
            )

    def units(buf, group):
        a, b = group
        m = 2 * (b - a) * unit_rows
        return jnp.concatenate([buf[a:b], buf[PAIRS + a : PAIRS + b]], axis=0).reshape(m, width)

    def hidden_rows(group):
        return pl.ds(2 * group[0] * unit_rows, 2 * (group[1] - group[0]) * unit_rows)

    def put_parts(group, v):
        a, b = group
        v = v.astype(BF16).reshape(2, b - a, unit_rows, width)
        part[a:b] = v[0]
        part[PAIRS + a : PAIRS + b] = v[1]

    def up(group):
        def go():
            r = hidden_rows(group)
            pre1[r, :] = dot_t(units(g1, group), w1[...])

            def act(i, _):
                s = pl.ds(pl.multiple_of(r.start + i * 32, 32), 32)
                hid[s, :] = gelu(pre1[s, :]).astype(BF16)
                return 0

            lax.fori_loop(0, r.size // 32, act, 0)

        return go

    def down(group):
        put_parts(group, dot(hid[hidden_rows(group), :], w2[...]))

    def up_back(group):
        def go():
            r = hidden_rows(group)
            hid[r, :] = (dot_t(units(g3, group), w2[...]) * pre1[r, :]).astype(BF16)

        return go

    def down_back(group):
        put_parts(group, dot(hid[hidden_rows(group), :], w1[...]))

    def scatter_mlp(phase, compute, idle):
        s = Scatter(phase)
        everything = pl.ds(0, unit_rows)
        compute(FAR)
        s.cross[FAR].start()
        s.cross[FAR].wait_recv()
        s.join(*FAR, everything)
        for q in QUARTERS:
            s.leave(q)
        compute(NEAR)
        s.cross[NEAR].start()
        s.cross[NEAR].wait_recv()
        s.join(*NEAR, everything)
        return s.relay(idle)

    near_row = iota((unit_rows, unit_rows), 0)
    far_row = iota((unit_rows, unit_rows), 1)

    def spread(a, b):
        return one_hot(far_row == lax.rem(near_row, a) * b + near_row // a)

    blocks = width // 128
    vgain[...] = line(vgain_ref, 0, blocks)
    v = dot(spread(merged_own, 4), x_ref[...])
    cen = v - jnp.mean(v, -1, keepdims=True)
    inv = lax.rsqrt(jnp.mean(cen * cen, -1, keepdims=True) + VIS_EPS)
    hat = cen * inv
    xhat[...] = hat
    xinv[...] = inv
    g1[0] = (hat * vgain[...]).astype(BF16)
    own[...] = v

    row = iota((1, dest_ref.size), 1)
    dest = line(dest_ref, 0, dest_ref.shape[0])
    dest_seq = jnp.zeros_like(dest)
    for n in range(1, 8):
        dest_seq += jnp.where(dest >= n * seq_len, 1, 0)
    inside = row & 31
    row_grp = row >> 7
    row_z = (row >> 5) & 3
    row_y = (row >> 4) & 1
    row_core = (row >> 3) & 1
    key = jnp.where(
        dest_seq == grp, ((row_grp & 6) | ((row_grp & 1) ^ row_y ^ yhi)) * 32 + inside, -1
    )
    token = (dest - dest_seq * seq_len + 1).astype(F32)
    tok = jnp.sum(jnp.where(key == iota((slots, row.shape[1]), 0), token, 0.0), -1, keepdims=True) - 1.0
    tcol[...] = tok.astype(jnp.int32)
    trow[...] = turned(tok).astype(jnp.int32)
    step_z = (row_z - z) & 3
    step_y = row_y ^ yhi
    pair = jnp.where(
        step_y == 0,
        jnp.where(step_z == 0, 0, jnp.where(step_z == 1, 1, jnp.where(step_z == 3, 2, 4))),
        jnp.where(step_z == 0, 3, jnp.where(step_z == 1, 5, jnp.where(step_z == 3, 6, 7))),
    )
    mine = ((row_grp >> 1) == x) & (((row_grp & 1) ^ row_y) == (ylo ^ yhi))
    key = jnp.where(mine, ((row_core ^ core) * PAIRS + pair) * merged_own + (row & 7), -1)
    slot = (dest_seq * 32 + inside).astype(F32)
    slot = jnp.sum(jnp.where(key == iota((merged_all, row.shape[1]), 0), slot, 0.0), -1, keepdims=True)
    scol[...] = slot.astype(jnp.int32)
    srow[...] = turned(slot).astype(jnp.int32)
    pl.semaphore_wait(barrier, 11)

    def exchange(src, dst, n):
        copies = []
        for k in range(1, 8):
            g, where = peer(k)
            copies.append(pltpu.make_async_remote_copy(
                src_ref=src.at[g], dst_ref=dst.at[grp],
                send_sem=esend.at[n, k - 1], recv_sem=erecv.at[n, k - 1],
                device_id=where, device_id_type=MESH,
            ))
        copies.append(pltpu.make_async_copy(src.at[grp], dst.at[grp], lsem.at[5 + n]))
        for copy in copies:
            copy.start()
        return copies

    def exchange_wait(copies):
        for copy in copies:
            copy.wait()

    holder = {}

    def pick():
        cot_load.wait()
        v = dot(one_hot(iota((slots, seq_len), 1) == tcol[...]), cot[...])
        picked[...] = v.astype(BF16).reshape(picked.shape)
        holder["cot"] = exchange(picked, returned, 0)

    def up_near():
        w1_load.wait()
        up(NEAR)()
        ls[...] = line(ls_ref, 0, blocks)
        for q in range(4):
            pgain[quarter(q), :] = jnp.broadcast_to(line(pgain_ref, q * blocks, blocks), (merged_own, width))

    def slopes():
        def act(i, _):
            r = pl.ds(pl.multiple_of(i * 32, 32), 32)
            pre1[r, :] = gelu_slope(pre1[r, :])
            return 0

        lax.fori_loop(0, UNITS, act, 0)

    gather(0, g1, pick, up_near, up(FAR))
    w2_load.wait()
    total = scatter_mlp(0, down, slopes)

    def over_merged(v):
        s = jnp.sum(v, -1, keepdims=True).reshape(4, merged_own, 1).sum(axis=0) * (1.0 / (4 * width))
        return jnp.concatenate([s] * 4, axis=0)

    y = (own[...] + ls[...] * total).astype(BF16).astype(F32)
    cen = y - over_merged(y)
    inv = lax.rsqrt(over_merged(cen * cen) + PROJ_EPS)
    hat = cen * inv
    mhat[...] = hat
    minv[...] = inv
    g2[0] = (hat * pgain[...]).astype(BF16)

    def ready():
        wp_load.wait()
        exchange_wait(holder["cot"])

    def project():
        free_part()
        for q in range(4):
            lhs = g2[:, quarter(q), :].reshape(merged_all, width)
            v = dot(lhs, wp[pl.ds(q * width, width), :])
            if q == 0:
                pre2[...] = v
            else:
                pre2[...] += v
        back = dot(one_hot(iota((merged_all, slots), 1) == scol[...]), returned[...].reshape(slots, -1))
        hid2[...] = (back * gelu_slope(pre2[...])).astype(BF16)

    def project_back(q):
        v = dot_t(hid2[...], wp[pl.ds(q * width, width), :])
        part[:, quarter(q), :] = v.astype(BF16).reshape(UNITS, merged_own, width)

    def send_projected():
        v = dot(one_hot(iota((slots, merged_all), 0) == srow[...]), gelu(pre2[...]).astype(BF16))
        out_slots[...] = v.astype(BF16).reshape(out_slots.shape)
        holder["proj"] = exchange(out_slots, arrived, 1)

    gather(1, g2, lambda: None, ready, project)
    s = Scatter(1)

    def far_ready(q):
        s.cross[q].wait_recv()
        s.join(*FAR, quarter(q))
        s.leave(q)

    for n, q in enumerate(QUARTERS):
        project_back(q)
        s.cross[q].start()
        if n:
            far_ready(QUARTERS[n - 1])
    far_ready(QUARTERS[3])
    s.join(*NEAR, pl.ds(0, unit_rows))
    total = s.relay(send_projected)
    hat = mhat[...]
    v = total * pgain[...]
    dm = minv[...] * (v - over_merged(v) - hat * over_merged(v * hat))
    dy = dm.astype(BF16).astype(F32)
    own[...] = dy
    g3[0] = (dy * ls[...]).astype(BF16)

    def fill():
        text_load.wait()
        exchange_wait(holder["proj"])
        block = 128
        flat = arrived[...].reshape(slots, -1)

        def step(i, _):
            r0 = pl.multiple_of(i * block, block)
            r = pl.ds(r0, block)
            hot = jnp.where(iota((block, slots), 0) + r0 == trow[...], 1.0, 0.0)
            v = dot(hot.astype(BF16), flat)
            filled = jnp.sum(hot, -1, keepdims=True) > 0.5
            seq[r, :] = jnp.where(filled, v, seq[r, :].astype(F32)).astype(BF16)
            return 0

        lax.fori_loop(0, seq_len // block, step, 0)
        holder["seq"] = pltpu.make_async_copy(seq, seq_hbm, lsem.at[7])
        holder["seq"].start()

    gather(2, g3, lambda: None, up_back(NEAR), up_back(FAR))
    free_part()
    total = scatter_mlp(2, down_back, fill)
    hat = xhat[...]
    v = total * vgain[...]
    g = own[...] + xinv[...] * (
        v - jnp.mean(v, -1, keepdims=True) - hat * jnp.mean(v * hat, -1, keepdims=True)
    )
    grad_ref[...] = dot(spread(4, merged_own), g.astype(BF16)).astype(BF16)
    free_part()
    holder["seq"].wait()


def junction(x, vgain, ls, pgain, dest, w1, w2, wp, text, cot):
    unit_rows, width = x.shape
    hidden = w1.shape[0]
    cols = wp.shape[1]
    all_rows = UNITS * unit_rows
    merged_all = all_rows // 4
    vmem = pl.BlockSpec(memory_space=pltpu.VMEM)
    hbm = pl.BlockSpec(memory_space=pl.ANY)
    V = pltpu.VMEM
    unit = (unit_rows, width)
    scratch = [
        V(w1.shape, BF16), V(w2.shape, BF16), V(wp.shape, BF16), V(cot.shape, BF16), V(text.shape, BF16),
        *[V((UNITS, *unit), BF16)] * 4,
        V((3, PAIRS, *unit), BF16),
        V((3, *unit), BF16), V((3, *unit), BF16), V((3, 2, *unit), BF16), V((3, *unit), BF16), V((3, 2, *unit), BF16),
        V((all_rows, hidden), F32), V((all_rows, hidden), BF16), V((merged_all, cols), F32), V((merged_all, cols), BF16),
        *[V((8, 32, cols), BF16)] * 4,
        V(unit, F32), V((unit_rows, 1), F32), V(unit, F32), V(unit, F32), V((unit_rows, 1), F32),
        V((1, width), F32), V((1, width), F32), V(unit, F32),
        V((merged_all, 1), jnp.int32), V((1, merged_all), jnp.int32), V((256, 1), jnp.int32), V((1, 256), jnp.int32),
        pltpu.SemaphoreType.DMA((3 * PHASE_MSGS,)), pltpu.SemaphoreType.DMA((3 * PHASE_MSGS,)),
        pltpu.SemaphoreType.DMA((2, 7)), pltpu.SemaphoreType.DMA((2, 7)),
        pltpu.SemaphoreType.DMA((8,)),
    ]
    return pl.pallas_call(
        kernel,
        out_shape=(jax.ShapeDtypeStruct(text.shape, BF16), jax.ShapeDtypeStruct(x.shape, BF16)),
        in_specs=[vmem] * 5 + [hbm] * 5,
        out_specs=(hbm, vmem),
        scratch_shapes=scratch,
        name="junction",
        compiler_params=pltpu.CompilerParams(
            collective_id=0, has_side_effects=True, vmem_limit_bytes=67_000_000
        ),
    )(x, vgain, ls, pgain, dest, w1, w2, wp, text, cot)


def per_device(
    vision_in, vis_gain, first_weight, second_weight, layer_scale,
    proj_gain, proj_weight, text_embed, dest_row, cotangent,
):
    return junction(
        vision_in, vis_gain.reshape(-1, 128), layer_scale.reshape(-1, 128), proj_gain.reshape(-1, 128),
        dest_row.reshape(-1, 128), first_weight.T, second_weight, proj_weight, text_embed, cotangent,
    )


def solution(mesh):
    torus = Mesh(mesh.devices.reshape(4, 2, 4, 2, 2), AXES)
    in_specs = (
        P((*GRP, *TP), None), P(), P(None, TP), P(TP, None), P(), P(), P(None, TP),
        P(GRP, TP), P(), P(GRP, TP),
    )
    out_specs = (P(GRP, TP), P((*GRP, *TP), None))
    return jax.shard_map(per_device, mesh=torus, in_specs=in_specs, out_specs=out_specs, check_vma=False)
```

profile of v0, /device:TPU:1, one launch (start us, length us, event | category | flops | bytes accessed | tf_op | source)
XLA Modules:
  0.0 125.3 jit_solution(16235515091734263028)
XLA Ops:
  0.6 121.6 %junction.1 = (bf16[1152,512]{1,0:T(8,128)(2,1)}, bf16[32,3200]{1,0:T(8,128)(2,1)}) custom-call(bf16[32,3200]{1,0:T(8,128)(2,1)} %x_ref.1, f32[25,128]{1,0:T(8,128)} %bitcast.7, f32[25,128]{1,0:T(8,128)} %bitcast.8, f32[100,128]{1,0:T(8,128)} %bitcast.6, s32[8,128]{1,0:T(8,128)} %bitcast.9, bf16[800,3200]{1,0:T(8,128)(2,1)} %bitcast.5, ...), custom_call_target="tpu_custom_call" | custom-call | tf_op jit(solution)/shard_map/junction/pallas_call | solution.py:551
  122.2 0.0 copy-start
  122.2 2.4 %copy.14 = bf16[1152,512]{1,0:T(8,128)(2,1)} copy(bf16[1152,512]{1,0:T(8,128)(2,1)} %get-tuple-element.4) | data formatting | bytes 2359296
  124.6 0.0 copy-done
  124.6 0.7 copy.15
Async XLA Ops:
  122.2 2.4 %copy-start = (bf16[32,3200]{1,0:T(8,128)(2,1)S(1)}, bf16[32,3200]{1,0:T(8,128)(2,1)}, u32[]{:S(2)}) copy-start(bf16[32,3200]{1,0:T(8,128)(2,1)} %get-tuple-element.5) | copy-start | bytes 614404
where the time goes:
time: 125 us
  Pallas kernels  122 us (98%)
  local copies, waits for them, and re-layouts  3.08 us (2%)
    pallas_call x1, Pallas kernels, junction(): pl.pallas_call(kernel, out_shape=(jax.ShapeDtypeStruct(text.shape, BF16),...  122 us
    unnamed x4, local copies, waits for them, and re-layouts  3.08 us

commit v1 on v0

--- a/solution.py
+++ b/solution.py
@@ -24,7 +24,7 @@
 NEAR = (0, 5)
 FAR = (5, 8)
 QUARTERS = (0, 3, 1, 2)
-AG_MSGS = 29
+AG_MSGS = 30
 RS_MSGS = 32
 PHASE_MSGS = AG_MSGS + RS_MSGS
 
@@ -72,7 +72,7 @@
     seq_hbm, grad_ref,
     w1, w2, wp, cot, seq,
     g1, g2, g3, part, rcore, rya, rye, rzb, rzc, rzd,
-    pre1, hid, pre2, hid2,
+    pre1, hid, pre2, hid2, back,
     out_slots, arrived, picked, returned,
     xhat, xinv, own, mhat, minv, vgain, ls, pgain,
     scol, srow, tcol, trow,
@@ -135,7 +135,7 @@
     def quarter(q):
         return pl.ds(q * merged_own, merged_own)
 
-    def gather(phase, buf, early, middle, late):
+    def gather(phase, buf, middle, late):
         count = iter(range(phase * PHASE_MSGS, phase * PHASE_MSGS + AG_MSGS))
 
         def msg(src, dst, where, rows=None):
@@ -144,8 +144,10 @@
                 s, d = s.at[rows], d.at[rows]
             return remote(s, d, where, next(count))
 
-        def cross(first, last):
-            return remote(buf.at[first:last], buf.at[PAIRS + first : PAIRS + last], "c", next(count))
+        def cross(first, last, rows=pl.ds(0, unit_rows)):
+            return remote(
+                buf.at[first:last, rows], buf.at[PAIRS + first : PAIRS + last, rows], "c", next(count)
+            )
 
         own_zp = [msg((0, 0), (-1, 0), "z+", quarter(q)) for q in range(4)]
         own_zm = [msg((0, 0), (1, 0), "z-", quarter(q)) for q in range(4)]
@@ -155,14 +157,13 @@
         y_zp = [msg((0, 1), (-1, 1), "z+", halves(h)) for h in range(2)]
         y_zm = [msg((0, 1), (1, 1), "z-", halves(h)) for h in range(2)]
         two_y = [msg((2, 0), (2, 1), "y", quarter(q)) for q in range(4)]
-        c_own, c_side, c_y, c_two, c_far, c_last = (
-            cross(*r) for r in ((0, 1), (1, 3), (3, 4), (4, 5), (5, 7), (7, 8))
-        )
+        c_own, c_side, c_y, c_two = (cross(*r) for r in ((0, 1), (1, 3), (3, 4), (4, 5)))
+        c_far = [cross(5, 7, halves(h)) for h in range(2)]
+        c_last = [cross(7, 8, halves(h)) for h in range(2)]
         for copy in (
             own_zp[0], own_zm[3], own_y[0], own_zp[1], own_zm[2], own_y[1], own_zp[2], own_zm[1], c_own,
         ):
             copy.start()
-        early()
         for p, m in ((0, 3), (1, 2)):
             own_zp[p].wait_recv()
             two[p].start()
@@ -173,14 +174,13 @@
         own_y[0].wait_recv()
         y_zp[0].start()
         y_zm[0].start()
-        for q in (0, 3):
-            two[q].wait_recv()
-            two_y[q].start()
+        two[0].wait_recv()
+        two_y[0].start()
         own_y[1].wait_recv()
         y_zp[1].start()
         y_zm[1].start()
         c_y.start()
-        for q in (1, 2):
+        for q in (1, 3, 2):
             two[q].wait_recv()
             two_y[q].start()
         c_two.start()
@@ -189,15 +189,16 @@
         c_side.start()
         for copy in (c_own, c_y, c_two, c_side):
             copy.wait_recv()
-        middle()
-        for copy in (*y_zp, *y_zm):
+        for h in range(2):
+            middle(h)
+            y_zp[h].wait_recv()
+            y_zm[h].wait_recv()
+            c_far[h].start()
+            for q in (2 * h, 2 * h + 1):
+                two_y[q].wait_recv()
+            c_last[h].start()
+        for copy in (*c_far, *c_last):
             copy.wait_recv()
-        c_far.start()
-        for copy in two_y:
-            copy.wait_recv()
-        c_last.start()
-        c_far.wait_recv()
-        c_last.wait_recv()
         late()
 
     class Scatter:
@@ -217,7 +218,7 @@
                 self.cross = [cross(0, PAIRS, quarter(q)) for q in range(4)]
             else:
                 everything = pl.ds(0, unit_rows)
-                self.cross = {g: cross(*g, everything) for g in (FAR, NEAR)}
+                self.cross = {g: cross(*g, everything) for g in ((5, 7), (7, 8), (4, 5), (1, 4), (0, 1))}
             self.a = [msg((2, 1), quarter(q), rya.at[phase], "y") for q in range(4)]
             self.b = [
                 (msg((1, 1), quarter(q), rzb.at[phase, 0], "z+"), msg((-1, 1), quarter(q), rzb.at[phase, 1], "z-"))
@@ -240,36 +241,32 @@
                 v = v + ref[rows, :].astype(F32)
             part[n, rows, :] = v.astype(BF16)
 
+        def joined(self, group):
+            self.cross[group].wait_recv()
+            self.join(*group, pl.ds(0, unit_rows))
+
         def leave(self, q):
             self.a[q].start()
             for copy in self.b[q]:
                 copy.start()
 
-        def relay(self, idle):
+        def early_side(self, q):
+            (self.dm if q < 2 else self.dp)[q].start()
+
+        def pass_two(self, q):
+            self.a[q].wait_recv()
+            self.add((2, 0), quarter(q), rya.at[self.phase])
+            self.c[q].start()
+
+        def pass_y(self, h):
+            for q in (2 * h, 2 * h + 1):
+                for copy in self.b[q]:
+                    copy.wait_recv()
+            self.add((0, 1), halves(h), rzb.at[self.phase, 0], rzb.at[self.phase, 1])
+            self.e[h].start()
+
+        def finish(self, idle):
             p = self.phase
-
-            def pass_two(q):
-                self.a[q].wait_recv()
-                self.add((2, 0), quarter(q), rya.at[p])
-                self.c[q].start()
-
-            def pass_y(h):
-                for q in (2 * h, 2 * h + 1):
-                    for copy in self.b[q]:
-                        copy.wait_recv()
-                self.add((0, 1), halves(h), rzb.at[p, 0], rzb.at[p, 1])
-                self.e[h].start()
-
-            pass_two(0)
-            pass_two(3)
-            pass_y(0)
-            pass_two(1)
-            pass_two(2)
-            for q in (2, 3):
-                self.dp[q].start()
-            for q in (1, 0):
-                self.dm[q].start()
-            pass_y(1)
             for q in QUARTERS:
                 self.c[q].wait_recv()
                 side, out = ((1, 0), self.dp) if q < 2 else ((-1, 0), self.dm)
@@ -296,47 +293,62 @@
         part[a:b] = v[0]
         part[PAIRS + a : PAIRS + b] = v[1]
 
-    def up(group):
-        def go():
-            r = hidden_rows(group)
-            pre1[r, :] = dot_t(units(g1, group), w1[...])
-
-            def act(i, _):
-                s = pl.ds(pl.multiple_of(r.start + i * 32, 32), 32)
-                hid[s, :] = gelu(pre1[s, :]).astype(BF16)
-                return 0
-
-            lax.fori_loop(0, r.size // 32, act, 0)
-
-        return go
+    lanes = [pl.ds(0, 512), pl.ds(512, w1.shape[0] - 512)]
+    all_lanes = pl.ds(0, w1.shape[0])
+
+    def up(group, lanes):
+        pre1[hidden_rows(group), lanes] = dot_t(units(g1, group), w1[lanes, :])
+
+    def activate(group):
+        r = hidden_rows(group)
+
+        def act(i, _):
+            s = pl.ds(pl.multiple_of(r.start + i * 32, 32), 32)
+            hid[s, :] = gelu(pre1[s, :]).astype(BF16)
+            return 0
+
+        lax.fori_loop(0, r.size // 32, act, 0)
 
     def down(group):
         put_parts(group, dot(hid[hidden_rows(group), :], w2[...]))
 
-    def up_back(group):
-        def go():
-            r = hidden_rows(group)
-            hid[r, :] = (dot_t(units(g3, group), w2[...]) * pre1[r, :]).astype(BF16)
-
-        return go
+    def up_back(group, lanes):
+        r = hidden_rows(group)
+        hid[r, lanes] = (dot_t(units(g3, group), w2[lanes, :]) * pre1[r, lanes]).astype(BF16)
 
     def down_back(group):
         put_parts(group, dot(hid[hidden_rows(group), :], w1[...]))
 
-    def scatter_mlp(phase, compute, idle):
+    def scatter_mlp(phase, compute, aside, idle):
         s = Scatter(phase)
-        everything = pl.ds(0, unit_rows)
         compute(FAR)
-        s.cross[FAR].start()
-        s.cross[FAR].wait_recv()
-        s.join(*FAR, everything)
+        s.cross[5, 7].start()
+        s.cross[7, 8].start()
+        aside()
+        s.joined((5, 7))
         for q in QUARTERS:
-            s.leave(q)
+            for copy in s.b[q]:
+                copy.start()
+        s.joined((7, 8))
+        for q in QUARTERS:
+            s.a[q].start()
         compute(NEAR)
-        s.cross[NEAR].start()
-        s.cross[NEAR].wait_recv()
-        s.join(*NEAR, everything)
-        return s.relay(idle)
+        for group in ((4, 5), (1, 4), (0, 1)):
+            s.cross[group].start()
+        s.joined((4, 5))
+        s.pass_two(0)
+        s.pass_two(3)
+        s.joined((1, 4))
+        s.early_side(0)
+        s.pass_two(1)
+        s.early_side(3)
+        s.pass_y(0)
+        s.pass_two(2)
+        s.early_side(1)
+        s.early_side(2)
+        s.joined((0, 1))
+        s.pass_y(1)
+        return s.finish(idle)
 
     near_row = iota((unit_rows, unit_rows), 0)
     far_row = iota((unit_rows, unit_rows), 1)
@@ -413,12 +425,19 @@
         picked[...] = v.astype(BF16).reshape(picked.shape)
         holder["cot"] = exchange(picked, returned, 0)
 
-    def up_near():
-        w1_load.wait()
-        up(NEAR)()
-        ls[...] = line(ls_ref, 0, blocks)
-        for q in range(4):
-            pgain[quarter(q), :] = jnp.broadcast_to(line(pgain_ref, q * blocks, blocks), (merged_own, width))
+    def up_near(h):
+        if h == 0:
+            w1_load.wait()
+        up(NEAR, lanes[h])
+        if h == 1:
+            activate(NEAR)
+            ls[...] = line(ls_ref, 0, blocks)
+            for q in range(4):
+                pgain[quarter(q), :] = jnp.broadcast_to(line(pgain_ref, q * blocks, blocks), (merged_own, width))
+
+    def up_far():
+        up(FAR, all_lanes)
+        activate(FAR)
 
     def slopes():
         def act(i, _):
@@ -428,9 +447,9 @@
 
         lax.fori_loop(0, UNITS, act, 0)
 
-    gather(0, g1, pick, up_near, up(FAR))
+    gather(0, g1, up_near, up_far)
     w2_load.wait()
-    total = scatter_mlp(0, down, slopes)
+    total = scatter_mlp(0, down, pick, slopes)
 
     def over_merged(v):
         s = jnp.sum(v, -1, keepdims=True).reshape(4, merged_own, 1).sum(axis=0) * (1.0 / (4 * width))
@@ -444,9 +463,11 @@
     minv[...] = inv
     g2[0] = (hat * pgain[...]).astype(BF16)
 
-    def ready():
-        wp_load.wait()
-        exchange_wait(holder["cot"])
+    def ready(h):
+        if h == 0:
+            wp_load.wait()
+            exchange_wait(holder["cot"])
+            back[...] = dot(one_hot(iota((merged_all, slots), 1) == scol[...]), returned[...].reshape(slots, -1))
 
     def project():
         free_part()
@@ -457,8 +478,7 @@
                 pre2[...] = v
             else:
                 pre2[...] += v
-        back = dot(one_hot(iota((merged_all, slots), 1) == scol[...]), returned[...].reshape(slots, -1))
-        hid2[...] = (back * gelu_slope(pre2[...])).astype(BF16)
+        hid2[...] = (back[...] * gelu_slope(pre2[...])).astype(BF16)
 
     def project_back(q):
         v = dot_t(hid2[...], wp[pl.ds(q * width, width), :])
@@ -469,22 +489,27 @@
         out_slots[...] = v.astype(BF16).reshape(out_slots.shape)
         holder["proj"] = exchange(out_slots, arrived, 1)
 
-    gather(1, g2, lambda: None, ready, project)
+    gather(1, g2, ready, project)
     s = Scatter(1)
 
-    def far_ready(q):
+    def joined(q):
         s.cross[q].wait_recv()
-        s.join(*FAR, quarter(q))
+        s.join(0, PAIRS, quarter(q))
         s.leave(q)
+        s.early_side(q)
 
     for n, q in enumerate(QUARTERS):
         project_back(q)
         s.cross[q].start()
         if n:
-            far_ready(QUARTERS[n - 1])
-    far_ready(QUARTERS[3])
-    s.join(*NEAR, pl.ds(0, unit_rows))
-    total = s.relay(send_projected)
+            joined(QUARTERS[n - 1])
+    s.pass_two(0)
+    joined(QUARTERS[3])
+    for q in QUARTERS[1:]:
+        s.pass_two(q)
+        if q != 3:
+            s.pass_y(q - 1)
+    total = s.finish(send_projected)
     hat = mhat[...]
     v = total * pgain[...]
     dm = minv[...] * (v - over_merged(v) - hat * over_merged(v * hat))
@@ -511,9 +536,9 @@
         holder["seq"] = pltpu.make_async_copy(seq, seq_hbm, lsem.at[7])
         holder["seq"].start()
 
-    gather(2, g3, lambda: None, up_back(NEAR), up_back(FAR))
+    gather(2, g3, lambda h: up_back(NEAR, lanes[h]), lambda: up_back(FAR, all_lanes))
     free_part()
-    total = scatter_mlp(2, down_back, fill)
+    total = scatter_mlp(2, down_back, lambda: None, fill)
     hat = xhat[...]
     v = total * vgain[...]
     g = own[...] + xinv[...] * (
@@ -540,6 +565,7 @@
         V((3, PAIRS, *unit), BF16),
         V((3, *unit), BF16), V((3, *unit), BF16), V((3, 2, *unit), BF16), V((3, *unit), BF16), V((3, 2, *unit), BF16),
         V((all_rows, hidden), F32), V((all_rows, hidden), BF16), V((merged_all, cols), F32), V((merged_all, cols), BF16),
+        V((merged_all, cols), F32),
         *[V((8, 32, cols), BF16)] * 4,
         V(unit, F32), V((unit_rows, 1), F32), V(unit, F32), V(unit, F32), V((unit_rows, 1), F32),
         V((1, width), F32), V((1, width), F32), V(unit, F32),
@@ -561,14 +587,48 @@
     )(x, vgain, ls, pgain, dest, w1, w2, wp, text, cot)
 
 
+def leave_kernel(seq_in, grad_in, seq_out, grad_out, seq, grad, sem_in, sem_out):
+    parts = sem_in.shape[0] - 1
+    rows = seq.shape[0] // parts
+    moves = [(grad_in, grad, grad_out)]
+    for n in range(parts):
+        r = pl.ds(n * rows, rows)
+        moves.append((seq_in.at[r], seq.at[r], seq_out.at[r]))
+    take = [pltpu.make_async_copy(src, mid, sem_in.at[n]) for n, (src, mid, _) in enumerate(moves)]
+    give = [pltpu.make_async_copy(mid, dst, sem_out.at[n]) for n, (_, mid, dst) in enumerate(moves)]
+    for copy in take:
+        copy.start()
+    for first, second in zip(take, give):
+        first.wait()
+        second.start()
+    for copy in give:
+        copy.wait()
+
+
+def leave(seq, grad):
+    hbm = pl.BlockSpec(memory_space=pl.ANY)
+    parts = 6
+    return pl.pallas_call(
+        leave_kernel,
+        out_shape=(jax.ShapeDtypeStruct(seq.shape, BF16), jax.ShapeDtypeStruct(grad.shape, BF16)),
+        in_specs=[hbm, hbm],
+        out_specs=(hbm, hbm),
+        scratch_shapes=[
+            pltpu.VMEM(seq.shape, BF16), pltpu.VMEM(grad.shape, BF16),
+            pltpu.SemaphoreType.DMA((parts + 1,)), pltpu.SemaphoreType.DMA((parts + 1,)),
+        ],
+        name="leave",
+    )(seq, grad)
+
+
 def per_device(
     vision_in, vis_gain, first_weight, second_weight, layer_scale,
     proj_gain, proj_weight, text_embed, dest_row, cotangent,
 ):
-    return junction(
+    return leave(*junction(
         vision_in, vis_gain.reshape(-1, 128), layer_scale.reshape(-1, 128), proj_gain.reshape(-1, 128),
         dest_row.reshape(-1, 128), first_weight.T, second_weight, proj_weight, text_embed, cotangent,
-    )
+    ))
 
 
 def solution(mesh):

time: 125 us -> 124 us (level)
  local copies, waits for them, and re-layouts: 3.08 us -> 0 us
    unnamed x4 -> x0, local copies, waits for them, and re-layouts: 3.08 us -> none
    pallas_call x0 -> x1, Pallas kernels: none -> 2.22 us  [leave(): pl.pallas_call(leave_kernel, out_shape=(jax.ShapeDtypeStruct(seq.shape, B...]
where the time goes in v1:
time: 124 us; the launch traced here: 123 us
  Pallas kernels  123 us (99%)
    pallas_call x1, Pallas kernels, junction(): pl.pallas_call(kernel, out_shape=(jax.ShapeDtypeStruct(text.shape, BF16),...  120 us

profile of v1, /device:TPU:1, one launch (start us, length us, event | category | flops | bytes accessed | tf_op | source)
XLA Modules:
  0.0 123.5 jit_solution(171086852407340912)
XLA Ops:
  0.6 120.4 %junction.1 = (bf16[1152,512]{1,0:T(8,128)(2,1)}, bf16[32,3200]{1,0:T(8,128)(2,1)}) custom-call(bf16[32,3200]{1,0:T(8,128)(2,1)} %x_ref.1, f32[25,128]{1,0:T(8,128)} %bitcast.7, f32[25,128]{1,0:T(8,128)} %bitcast.8, f32[100,128]{1,0:T(8,128)} %bitcast.6, s32[8,128]{1,0:T(8,128)} %bitcast.9, bf16[800,3200]{1,0:T(8,128)(2,1)} %bitcast.5, ...), custom_call_target="tpu_custom_call" | custom-call | tf_op jit(solution)/shard_map/junction/pallas_call | solution.py:577
  121.1 2.2 %leave.1 = (bf16[1152,512]{1,0:T(8,128)(2,1)}, bf16[32,3200]{1,0:T(8,128)(2,1)}) custom-call(bf16[1152,512]{1,0:T(8,128)(2,1)} %get-tuple-element.4.seq_in, bf16[32,3200]{1,0:T(8,128)(2,1)} %get-tuple-element.5.grad_in), custom_call_target="tpu_custom_call" | custom-call | tf_op jit(solution)/shard_map/leave/pallas_call | solution.py:611

commit v2 on v1

--- a/solution.py
+++ b/solution.py
@@ -72,7 +72,7 @@
     seq_hbm, grad_ref,
     w1, w2, wp, cot, seq,
     g1, g2, g3, part, rcore, rya, rye, rzb, rzc, rzd,
-    pre1, hid, pre2, hid2, back,
+    pre1, hid, pre2, hid2, back, half_sum,
     out_slots, arrived, picked, returned,
     xhat, xinv, own, mhat, minv, vgain, ls, pgain,
     scol, srow, tcol, trow,
@@ -135,31 +135,39 @@
     def quarter(q):
         return pl.ds(q * merged_own, merged_own)
 
-    def gather(phase, buf, middle, late):
+    edges = [width // 512 * 128 * n + (128 if n else 0) for n in range(4)] + [width]
+
+    def col_quarter(q):
+        return pl.ds(edges[q], edges[q + 1] - edges[q])
+
+    def col_half(h):
+        return pl.ds(edges[2 * h], edges[2 * h + 2] - edges[2 * h])
+
+    def gather(phase, buf, middle, tail, late):
         count = iter(range(phase * PHASE_MSGS, phase * PHASE_MSGS + AG_MSGS))
 
-        def msg(src, dst, where, rows=None):
+        def msg(src, dst, where, cols=None):
             s, d = buf.at[PAIR[src]], buf.at[PAIR[dst]]
-            if rows is not None:
-                s, d = s.at[rows], d.at[rows]
+            if cols is not None:
+                s, d = s.at[:, cols], d.at[:, cols]
             return remote(s, d, where, next(count))
 
-        def cross(first, last, rows=pl.ds(0, unit_rows)):
+        def cross(first, last, cols=pl.ds(0, width)):
             return remote(
-                buf.at[first:last, rows], buf.at[PAIRS + first : PAIRS + last, rows], "c", next(count)
+                buf.at[first:last, :, cols], buf.at[PAIRS + first : PAIRS + last, :, cols], "c", next(count)
             )
 
-        own_zp = [msg((0, 0), (-1, 0), "z+", quarter(q)) for q in range(4)]
-        own_zm = [msg((0, 0), (1, 0), "z-", quarter(q)) for q in range(4)]
-        own_y = [msg((0, 0), (0, 1), "y", halves(h)) for h in range(2)]
-        two = {q: msg((-1, 0), (2, 0), "z+", quarter(q)) for q in (0, 1)}
-        two |= {q: msg((1, 0), (2, 0), "z-", quarter(q)) for q in (3, 2)}
-        y_zp = [msg((0, 1), (-1, 1), "z+", halves(h)) for h in range(2)]
-        y_zm = [msg((0, 1), (1, 1), "z-", halves(h)) for h in range(2)]
-        two_y = [msg((2, 0), (2, 1), "y", quarter(q)) for q in range(4)]
+        own_zp = [msg((0, 0), (-1, 0), "z+", col_quarter(q)) for q in range(4)]
+        own_zm = [msg((0, 0), (1, 0), "z-", col_quarter(q)) for q in range(4)]
+        own_y = [msg((0, 0), (0, 1), "y", col_half(h)) for h in range(2)]
+        two = {q: msg((-1, 0), (2, 0), "z+", col_quarter(q)) for q in (0, 1)}
+        two |= {q: msg((1, 0), (2, 0), "z-", col_quarter(q)) for q in (3, 2)}
+        y_zp = [msg((0, 1), (-1, 1), "z+", col_half(h)) for h in range(2)]
+        y_zm = [msg((0, 1), (1, 1), "z-", col_half(h)) for h in range(2)]
+        two_y = [msg((2, 0), (2, 1), "y", col_quarter(q)) for q in range(4)]
         c_own, c_side, c_y, c_two = (cross(*r) for r in ((0, 1), (1, 3), (3, 4), (4, 5)))
-        c_far = [cross(5, 7, halves(h)) for h in range(2)]
-        c_last = [cross(7, 8, halves(h)) for h in range(2)]
+        c_far = [cross(5, 7, col_half(h)) for h in range(2)]
+        c_last = [cross(7, 8, col_half(h)) for h in range(2)]
         for copy in (
             own_zp[0], own_zm[3], own_y[0], own_zp[1], own_zm[2], own_y[1], own_zp[2], own_zm[1], c_own,
         ):
@@ -197,9 +205,10 @@
             for q in (2 * h, 2 * h + 1):
                 two_y[q].wait_recv()
             c_last[h].start()
-        for copy in (*c_far, *c_last):
-            copy.wait_recv()
-        late()
+        for h, step in ((0, tail), (1, late)):
+            c_far[h].wait_recv()
+            c_last[h].wait_recv()
+            step()
 
     class Scatter:
         def __init__(self, phase):
@@ -279,10 +288,11 @@
                 part[0].astype(F32) + rzd[p, 0].astype(F32) + rzd[p, 1].astype(F32) + rye[p].astype(F32)
             )
 
-    def units(buf, group):
+    def units(buf, group, cols=pl.ds(0, width)):
         a, b = group
         m = 2 * (b - a) * unit_rows
-        return jnp.concatenate([buf[a:b], buf[PAIRS + a : PAIRS + b]], axis=0).reshape(m, width)
+        both = jnp.concatenate([buf[a:b, :, cols], buf[PAIRS + a : PAIRS + b, :, cols]], axis=0)
+        return both.reshape(m, cols.size)
 
     def hidden_rows(group):
         return pl.ds(2 * group[0] * unit_rows, 2 * (group[1] - group[0]) * unit_rows)
@@ -293,8 +303,10 @@
         part[a:b] = v[0]
         part[PAIRS + a : PAIRS + b] = v[1]
 
-    lanes = [pl.ds(0, 512), pl.ds(512, w1.shape[0] - 512)]
-    all_lanes = pl.ds(0, w1.shape[0])
+    lanes = [[pl.ds(512, w1.shape[0] - 512)], [pl.ds(256, 256), pl.ds(0, 256)]]
+
+    def far_first(buf, weights, h):
+        return dot_t(units(buf, FAR, col_half(h)), weights[:, col_half(h)])
 
     def up(group, lanes):
         pre1[hidden_rows(group), lanes] = dot_t(units(g1, group), w1[lanes, :])
@@ -315,6 +327,13 @@
     def up_back(group, lanes):
         r = hidden_rows(group)
         hid[r, lanes] = (dot_t(units(g3, group), w2[lanes, :]) * pre1[r, lanes]).astype(BF16)
+
+    def up_back_far(h):
+        r = hidden_rows(FAR)
+        if h == 0:
+            half_sum[...] = far_first(g3, w2, 0)
+        else:
+            hid[r, :] = ((half_sum[...] + far_first(g3, w2, 1)) * pre1[r, :]).astype(BF16)
 
     def down_back(group):
         put_parts(group, dot(hid[hidden_rows(group), :], w1[...]))
@@ -428,16 +447,23 @@
     def up_near(h):
         if h == 0:
             w1_load.wait()
-        up(NEAR, lanes[h])
-        if h == 1:
-            activate(NEAR)
-            ls[...] = line(ls_ref, 0, blocks)
-            for q in range(4):
-                pgain[quarter(q), :] = jnp.broadcast_to(line(pgain_ref, q * blocks, blocks), (merged_own, width))
-
-    def up_far():
-        up(FAR, all_lanes)
-        activate(FAR)
+        for n in lanes[h]:
+            up(NEAR, n)
+
+    def up_far(h):
+        r = hidden_rows(FAR)
+        if h == 0:
+            pre1[r, :] = far_first(g1, w1, 0)
+        else:
+            pre1[r, :] += far_first(g1, w1, 1)
+            activate(FAR)
+
+    def after_first():
+        ls[...] = line(ls_ref, 0, blocks)
+        for q in range(4):
+            pgain[quarter(q), :] = jnp.broadcast_to(line(pgain_ref, q * blocks, blocks), (merged_own, width))
+        pick()
+        slopes()
 
     def slopes():
         def act(i, _):
@@ -447,9 +473,9 @@
 
         lax.fori_loop(0, UNITS, act, 0)
 
-    gather(0, g1, up_near, up_far)
+    gather(0, g1, up_near, lambda: up_far(0), lambda: up_far(1))
     w2_load.wait()
-    total = scatter_mlp(0, down, pick, slopes)
+    total = scatter_mlp(0, down, lambda: activate(NEAR), after_first)
 
     def over_merged(v):
         s = jnp.sum(v, -1, keepdims=True).reshape(4, merged_own, 1).sum(axis=0) * (1.0 / (4 * width))
@@ -469,16 +495,18 @@
             exchange_wait(holder["cot"])
             back[...] = dot(one_hot(iota((merged_all, slots), 1) == scol[...]), returned[...].reshape(slots, -1))
 
-    def project():
-        free_part()
+    def project(h):
         for q in range(4):
-            lhs = g2[:, quarter(q), :].reshape(merged_all, width)
-            v = dot(lhs, wp[pl.ds(q * width, width), :])
-            if q == 0:
+            cols = col_half(h)
+            lhs = g2[:, quarter(q), cols].reshape(merged_all, cols.size)
+            v = dot(lhs, wp[pl.ds(q * width + cols.start, cols.size), :])
+            if q == h == 0:
                 pre2[...] = v
             else:
                 pre2[...] += v
-        hid2[...] = (back[...] * gelu_slope(pre2[...])).astype(BF16)
+        if h == 1:
+            hid2[...] = (back[...] * gelu_slope(pre2[...])).astype(BF16)
+            free_part()
 
     def project_back(q):
         v = dot_t(hid2[...], wp[pl.ds(q * width, width), :])
@@ -489,7 +517,7 @@
         out_slots[...] = v.astype(BF16).reshape(out_slots.shape)
         holder["proj"] = exchange(out_slots, arrived, 1)
 
-    gather(1, g2, ready, project)
+    gather(1, g2, ready, lambda: project(0), lambda: project(1))
     s = Scatter(1)
 
     def joined(q):
@@ -536,7 +564,11 @@
         holder["seq"] = pltpu.make_async_copy(seq, seq_hbm, lsem.at[7])
         holder["seq"].start()
 
-    gather(2, g3, lambda h: up_back(NEAR, lanes[h]), lambda: up_back(FAR, all_lanes))
+    def back_near(h):
+        for n in lanes[h]:
+            up_back(NEAR, n)
+
+    gather(2, g3, back_near, lambda: up_back_far(0), lambda: up_back_far(1))
     free_part()
     total = scatter_mlp(2, down_back, lambda: None, fill)
     hat = xhat[...]
@@ -565,7 +597,7 @@
         V((3, PAIRS, *unit), BF16),
         V((3, *unit), BF16), V((3, *unit), BF16), V((3, 2, *unit), BF16), V((3, *unit), BF16), V((3, 2, *unit), BF16),
         V((all_rows, hidden), F32), V((all_rows, hidden), BF16), V((merged_all, cols), F32), V((merged_all, cols), BF16),
-        V((merged_all, cols), F32),
+        V((merged_all, cols), F32), V((2 * (FAR[1] - FAR[0]) * unit_rows, hidden), F32),
         *[V((8, 32, cols), BF16)] * 4,
         V(unit, F32), V((unit_rows, 1), F32), V(unit, F32), V(unit, F32), V((unit_rows, 1), F32),
         V((1, width), F32), V((1, width), F32), V(unit, F32),

time: 124 us -> 120 us (0.968)
  Pallas kernels: 123 us -> 119 us
    pallas_call x1, Pallas kernels: 120 us -> 117 us  [junction(): pl.pallas_call(kernel, out_shape=(jax.ShapeDtypeStruct(text.shape, BF16),...]
where the time goes in v2:
time: 120 us
  Pallas kernels  119 us (99%)
    pallas_call x1, Pallas kernels, junction(): pl.pallas_call(kernel, out_shape=(jax.ShapeDtypeStruct(text.shape, BF16),...  117 us

profile of v2, /device:TPU:1, one launch (start us, length us, event | category | flops | bytes accessed | tf_op | source)
XLA Modules:
  0.0 120.0 jit_solution(12314426254134976188)
XLA Ops:
  0.6 117.0 %junction.1 = (bf16[1152,512]{1,0:T(8,128)(2,1)}, bf16[32,3200]{1,0:T(8,128)(2,1)}) custom-call(bf16[32,3200]{1,0:T(8,128)(2,1)} %x_ref.1, f32[25,128]{1,0:T(8,128)} %bitcast.7, f32[25,128]{1,0:T(8,128)} %bitcast.8, f32[100,128]{1,0:T(8,128)} %bitcast.6, s32[8,128]{1,0:T(8,128)} %bitcast.9, bf16[800,3200]{1,0:T(8,128)(2,1)} %bitcast.5, ...), custom_call_target="tpu_custom_call" | custom-call | tf_op jit(solution)/shard_map/junction/pallas_call | solution.py:609
  117.6 2.2 %leave.1 = (bf16[1152,512]{1,0:T(8,128)(2,1)}, bf16[32,3200]{1,0:T(8,128)(2,1)}) custom-call(bf16[1152,512]{1,0:T(8,128)(2,1)} %get-tuple-element.4.seq_in, bf16[32,3200]{1,0:T(8,128)(2,1)} %get-tuple-element.5.grad_in), custom_call_target="tpu_custom_call" | custom-call | tf_op jit(solution)/shard_map/leave/pallas_call | solution.py:643
